TPU v7x, 32 devices: a whole 2x2x4 slice. The times are simulated.
32 devices in a mesh: grp: 4 (over y, core), ch: 8 (over z, x).
Axes of the slice: x: 2, y: 2, z: 4, core: 2. Of those that a mesh axis runs over, the one named last changes fastest.
Arguments:
- strain: bfloat16 [8, 1024, 4096], P('grp', 'ch'), may hold values from -6 to 6
- valid_mask: int32 [8, 1024], P('grp', 'ch'), may hold values 0 or 1
- pair_list: int32 [8, 6, 2], P('ch'), may hold values from 0 to 7, as said below
- owner_group: int32 [8, 6], P('ch'), may hold values from 0 to 3, as said below
Outputs:
- stacks: float32 [4, 8, 2, 128, 4096], P('grp', 'ch')
Inputs may be any that keep to these rules, and one draw needn't show every extreme that they name: `pair_list`: entries are channel block numbers; each ordered pair of blocks appears at most once over all columns. `owner_group`: in each column no group owns more than 2 entries, and some group owns exactly 2.
All inputs are finite; a program needn't handle non-finite values. No bound on the sum of `valid_mask` on one device may be relied on, other than what follows from the above.
Results may differ from a plain program's by a relative error of at most 0.0042.
Values may be sent and summed in bfloat16 or wider, within the bound.
A program may use at most 192 MiB of HBM per device.

v0:
```python
import math
import jax
import jax.numpy as jnp
from jax import lax
from jax.sharding import PartitionSpec as P

NFFT = 4096
NB = 1024
SUB = 64
BLK = 128
CAP = 2


def forward_table(length, bins):
    samples = jnp.arange(length, dtype=jnp.int32)
    frequency = jnp.arange(1, bins + 1, dtype=jnp.int32)
    angles = jnp.mod(samples[:, None] * frequency[None, :], length).astype(jnp.float32) * (
        2.0 * math.pi / length
    )
    hann_taper = 0.5 - 0.5 * jnp.cos(samples.astype(jnp.float32) * (2.0 * math.pi / length))
    return jnp.concatenate(
        [hann_taper[:, None] * jnp.cos(angles), -hann_taper[:, None] * jnp.sin(angles)], axis=1
    ).astype(jnp.bfloat16)


def inverse_table(length, bins):
    frequency = jnp.arange(1, bins + 1, dtype=jnp.int32)
    lag_index = jnp.arange(length, dtype=jnp.int32) - length // 2
    angles = jnp.mod(frequency[:, None] * lag_index[None, :], length).astype(jnp.float32) * (
        2.0 * math.pi / length
    )
    return jnp.concatenate([jnp.cos(angles), -jnp.sin(angles)], axis=0)


def whiten_rows(spectrum, valid_mask, bins, band):
    real_part = spectrum[..., :bins]
    imag_part = spectrum[..., bins:]
    power = real_part * real_part + imag_part * imag_part
    band_power = jnp.sum(power.reshape(power.shape[:-1] + (bins // band, band)), axis=-1) / band
    norm_full = jnp.repeat(jnp.sqrt(band_power + 1e-06), band, axis=-1)
    norm_both = jnp.concatenate([norm_full, norm_full], axis=-1)
    return (spectrum / norm_both * valid_mask[..., None].astype(jnp.float32)).astype(jnp.bfloat16)


def cross_block(rows, pair_entry, block, bins):
    first_rows = lax.dynamic_slice_in_dim(rows, pair_entry[0] * block, block, 1).astype(jnp.float32)
    second_rows = lax.dynamic_slice_in_dim(rows, pair_entry[1] * block, block, 1).astype(
        jnp.float32
    )
    first_real = first_rows[..., :bins]
    first_imag = first_rows[..., bins:]
    second_real = second_rows[..., :bins]
    second_imag = second_rows[..., bins:]
    cross_real = jnp.sum(first_real * second_real + first_imag * second_imag, axis=0)
    cross_imag = jnp.sum(first_real * second_imag - first_imag * second_real, axis=0)
    return jnp.concatenate([cross_real, cross_imag], axis=-1)


def local(strain, valid_mask, pair_list, owner_group):
    window_count = strain.shape[0]
    groups = lax.axis_size("grp")
    forward = forward_table(NFFT, NB)
    spectrum = jnp.dot(strain.reshape(-1, NFFT), forward, preferred_element_type=jnp.float32)
    spectrum = spectrum.reshape(strain.shape[0], strain.shape[1], 2 * NB)
    white = whiten_rows(spectrum, valid_mask, NB, SUB)
    gathered = lax.all_gather(white, "ch", axis=1, tiled=True)
    pair_codes = pair_list[0]
    partial_value = lax.map(
        lambda pair_entry: cross_block(gathered, pair_entry, BLK, NB), pair_codes
    )
    owners = owner_group[0]
    list_len = owners.shape[0]
    positions = jnp.arange(list_len, dtype=jnp.int32)
    earlier = positions[None, :] < positions[:, None]
    slot_rank = jnp.sum(((owners[:, None] == owners[None, :]) & earlier).astype(jnp.int32), axis=1)
    slot_ids = jnp.arange(CAP, dtype=jnp.int32)
    flat_partial = partial_value.reshape(list_len, -1)
    summed = lax.psum(flat_partial, "grp")
    my_group = lax.axis_index("grp")
    picking = ((owners[None, :] == my_group) & (slot_rank[None, :] == slot_ids[:, None])).astype(
        jnp.float32
    )
    total = jnp.dot(
        picking, summed, precision=lax.Precision.HIGHEST, preferred_element_type=jnp.float32
    )
    inverse = inverse_table(NFFT, NB)
    stacked = jnp.dot(
        total.reshape(-1, 2 * NB),
        inverse,
        precision=lax.Precision.HIGHEST,
        preferred_element_type=jnp.float32,
    )
    scale = 1.0 / math.sqrt(NB * window_count * groups)
    return (stacked * scale).reshape(1, 1, CAP, BLK, NFFT)


def solution(mesh):
    placed = (P("grp", "ch", None), P("grp", "ch"), P("ch", None, None), P("ch", None))
    return jax.shard_map(
        local,
        mesh=mesh,
        in_specs=placed,
        out_specs=P("grp", "ch", None, None, None),
        check_vma=False,
    )
```

profile of v0, /device:TPU:0, one launch (start us, length us, event | category | flops | bytes accessed | tf_op | source)
XLA Modules:
  0.0 475.3 jit_solution(4424673960620839761)
XLA Ops:
  6.5 0.1 multiply_subtract_fusion
  6.6 0.8 convert_element_type.43
  7.4 69.9 %multiply_convert_fusion.1 = (bf16[4096,1024]{1,0:T(8,128)(2,1)}, bf16[4096,1024]{1,0:T(8,128)(2,1)}) fusion(s32[1024]{0:T(1024)S(1)} %iota_add_fusion.1, f32[4096]{0:T(1024)S(1)} %get-tuple-element.54, f32[4096]{0:T(1024)S(1)} %get-tuple-element.55), kind=kLoop, calls=%fused_computation.31 | loop fusion | flops 75497472 | bytes 16814080 | tf_op jit(solution)/shard_map/convert
  77.4 9.8 %fusion.11 = f32[2048,256]{0,1:T(8,128)} fusion(bf16[256,4096]{1,0:T(8,128)(2,1)S(1)} %bitcast.29, bf16[4096,1024]{1,0:T(8,128)(2,1)} %get-tuple-element.53, bf16[4096,1024]{1,0:T(8,128)(2,1)} %get-tuple-element.52), kind=kOutput, calls=%fused_computation.25 | convolution fusion | flops 4328521728 | bytes 20971520 | tf_op jit(solution)/shard_map/dot_general | solution.py:63
  87.2 1.9 copy.11
  89.1 0.2 bitcast_reduce_fusion
  89.5 1.2 fusion.23
  90.7 0.2 all-reduce.2.cloned.1.call-start
  91.0 127.6 %all-gather.2.cloned.1.call-done = bf16[2,1024,2048]{1,2,0:T(8,128)(2,1)} async-done(((bf16[2,128,2048]{1,2,0:T(8,128)(2,1)}), bf16[2,1024,2048]{1,2,0:T(8,128)(2,1)}) %all-gather.2.cloned.1.call-update) | async-done | bytes 8388624 | tf_op jit(solution)/shard_map/all_gather | solution.py:66
  218.5 11.7 %copy.12 = bf16[2,1024,2048]{2,1,0:T(8,128)(2,1)} copy(bf16[2,1024,2048]{1,2,0:T(8,128)(2,1)} %all-gather.2.cloned.1.call-done) | data formatting | bytes 16777216 | tf_op jit(solution)/shard_map/while | solution.py:68
  230.2 32.5 %while.10 = (s32[]{:T(128)}, f32[6,128,2048]{2,1,0:T(8,128)}, s32[6,2]{0,1:T(2,128)S(1)}, bf16[2,1024,2048]{2,1,0:T(8,128)(2,1)}, s32[]{:T(128)}, /*index=5*/s32[1,1]{0,1:T(1,128)}, s32[]{:T(128)}, s32[]{:T(128)}) while((s32[]{:T(128)}, f32[6,128,2048]{2,1,0:T(8,128)}, s32[6,2]{0,1:T(2,128)S(1)}, bf16[2,1024,2048]{2,1,0:T(8,128)(2,1)}, ...), condition=%wide.region_5.6_spmd, body=%wide.region_2.0_spmd.sunk | while | flops 3145738 | bytes 13631721 | solution.py:68
  230.2 0.1 constant_dynamic-slice_fusion.2
  230.3 0.5 fusion.41
  232.1 1.9 dynamic-slice_convert_fusion.3
  234.0 0.6 add_reduce_fusion.2
  234.6 1.1 fusion.42
  235.6 0.1 constant_dynamic-slice_fusion.2
  235.7 0.5 fusion.41
  237.5 1.9 dynamic-slice_convert_fusion.3
  239.4 0.6 add_reduce_fusion.2
  240.0 1.1 fusion.42
  241.1 0.1 constant_dynamic-slice_fusion.2
  241.1 0.5 fusion.41
  242.9 1.9 dynamic-slice_convert_fusion.3
  244.8 0.6 add_reduce_fusion.2
  245.4 1.1 fusion.42
  246.5 0.1 constant_dynamic-slice_fusion.2
  246.6 0.5 fusion.41
  248.4 1.9 dynamic-slice_convert_fusion.3
  250.3 0.6 add_reduce_fusion.2
  250.8 1.1 fusion.42
  251.9 0.1 constant_dynamic-slice_fusion.2
  252.0 0.5 fusion.41
  253.8 1.9 dynamic-slice_convert_fusion.3
  255.7 0.6 add_reduce_fusion.2
  256.2 1.1 fusion.42
  257.3 0.1 constant_dynamic-slice_fusion.2
  257.3 0.5 fusion.41
  259.2 1.9 dynamic-slice_convert_fusion.3
  261.0 0.6 add_reduce_fusion.2
  261.6 1.1 fusion.42
  262.7 9.8 %copy.13 = f32[1,6,128,2048]{3,1,2,0:T(8,128)} copy(f32[1,6,128,2048]{3,2,1,0:T(8,128)} %bitcast.31) | data formatting | bytes 12582912
  272.5 0.2 convert_reduce_fusion
  272.7 68.4 %fusion.18 = (f32[1024,4096]{1,0:T(8,128)}, f32[1024,4096]{1,0:T(8,128)}) fusion(s32[4096]{0:T(1024)S(1)} %iota_add_fusion, s32[1024]{0:T(1024)S(1)} %iota_add_fusion.1), kind=kLoop, calls=%fused_computation.35 | loop fusion | flops 62914560 | bytes 33574912 | tf_op jit(solution)/shard_map/cos | solution.py:32
  341.2 82.5 %all-reduce.2.cloned.1.call-done = f32[6,262144]{1,0:T(8,128)} async-done(((f32[6,262144]{1,0:T(8,128)}), f32[6,262144]{1,0:T(8,128)}) %all-reduce.2.cloned.1.call-update) | async-done | bytes 6291472 | tf_op jit(solution)/shard_map/psum | solution.py:78
  423.7 7.4 %fusion.27 = f32[2,262144]{1,0:T(2,128)S(1)} fusion(f32[6,262144]{1,0:T(8,128)} %all-reduce.2.cloned.1.call-done, pred[6]{0:T(512)(128)(4,1)S(1)} %compare_bitcast_fusion, s32[6]{0:T(128)S(1)} %convert_reduce_fusion), kind=kOutput, calls=%fused_computation.52 | convolution fusion | flops 37748760 | bytes 8388638 | tf_op jit(solution)/shard_map/dot_general | solution.py:83
  431.1 3.1 reshape.62
  434.2 34.3 %fusion.19 = f32[256,4096]{1,0:T(8,128)} fusion(f32[256,2048]{1,0:T(8,128)} %reshape.62, f32[1024,4096]{1,0:T(8,128)} %get-tuple-element.51, f32[1024,4096]{1,0:T(8,128)} %get-tuple-element.50), kind=kOutput, calls=%fused_computation.36 | convolution fusion | flops 25779240960 | bytes 39845888 | tf_op jit(solution)/shard_map/dot_general | solution.py:87
  (17 shorter events, 0.1 us)
Async XLA Ops:
  6.5 70.9 %copy-start = (bf16[2,128,4096]{2,1,0:T(8,128)(2,1)S(1)}, bf16[2,128,4096]{2,1,0:T(8,128)(2,1)}, u32[]{:S(2)}) copy-start(bf16[2,128,4096]{2,1,0:T(8,128)(2,1)} %param.6) | copy-start | bytes 6291460
  6.5 212.0 %all-gather.2.cloned.1.call-start = ((), (), s32[]{:S(2)}) async-start(), calls=%async_computation | async-start | bytes 9437184 | tf_op jit(solution)/shard_map/all_gather | solution.py:66
  90.7 333.0 %all-reduce.2.cloned.1.call-start = ((), (), s32[]{:S(2)}) async-start(), calls=%async_computation.1 | async-start | bytes 16777216 | tf_op jit(solution)/shard_map/psum | solution.py:78
  91.0 139.3 %copy-start.2 = (s32[1,6,2]{1,2,0:T(2,128)S(1)}, s32[1,6,2]{1,2,0:T(2,128)}, u32[]{:S(2)}) copy-start(s32[1,6,2]{1,2,0:T(2,128)} %param.8) | copy-start | bytes 148
  262.7 9.8 %copy-start.3 = (s32[1,6]{1,0:T(1,128)S(1)}, s32[1,6]{1,0:T(1,128)}, u32[]{:S(2)}) copy-start(s32[1,6]{1,0:T(1,128)} %param.9) | copy-start | bytes 76
  434.2 34.3 %copy-start.1 = (bf16[2,128,4096]{2,1,0:T(8,128)(2,1)S(1)}, bf16[2,128,4096]{2,1,0:T(8,128)(2,1)}, u32[]{:S(2)}) copy-start(bf16[2,128,4096]{2,1,0:T(8,128)(2,1)} %param.6) | copy-start | bytes 6291460
Sparse Core Ops, SparseCore 0:
  90.9 127.6 all-gather.1
  272.6 151.0 all-reduce.1
where the time goes:
time: 476 us; the launch traced here: 475 us
  waiting for transfers between devices  210 us (44%)
  other arithmetic  162 us (34%)
  matrix products  51.5 us (11%)
  local copies, waits for them, and re-layouts  30.2 us (6%)
  between operations  13.5 us (3%)
  loops' own time  7.78 us (2%)
    all_gather x1, waiting for transfers between devices, local(): gathered = lax.all_gather(white, 'ch', axis=1, tiled=True)  128 us
    psum x1, waiting for transfers between devices, local(): summed = lax.psum(flat_partial, 'grp')  82.5 us
    another operation x1, other arithmetic  69.9 us
    cos x1, other arithmetic, inverse_table(): return jnp.concatenate([jnp.cos(angles), -jnp.sin(angles)], axis=0)  68.4 us
    dot_general x1, matrix products, local(): jnp.dot(total.reshape(-1, 2 * NB), inverse, precision=lax.Precision.HIGHE...  34.3 us
    while x1, local copies, waits for them, and re-layouts, local(): lax.map(lambda pair_entry: cross_block(gathered, pair_entry, BLK, NB), pa...  11.7 us
    convert_element_type x6, other arithmetic, cross_block(): lax.dynamic_slice_in_dim(rows, pair_entry[0] * block, block, 1)  11.3 us
    dot_general x1, matrix products, local(): jnp.dot(strain.reshape(-1, NFFT), forward, preferred_element_type=jnp.flo...  9.8 us
  transfers between devices with their start and end apart: 2, of which 2 were waited for; matrix products, arithmetic and copies ran while one was open for 14% of the time, Pallas kernels for 0%

commit v1 on v0

--- a/solution.py
+++ b/solution.py
@@ -63,7 +63,24 @@
     spectrum = jnp.dot(strain.reshape(-1, NFFT), forward, preferred_element_type=jnp.float32)
     spectrum = spectrum.reshape(strain.shape[0], strain.shape[1], 2 * NB)
     white = whiten_rows(spectrum, valid_mask, NB, SUB)
-    gathered = lax.all_gather(white, "ch", axis=1, tiled=True)
+    size, index, rows_2 = (lax.axis_size("ch"), lax.axis_index("ch"), white.shape[1])
+    forward_2 = [(i, (i + 1) % size) for i in range(size)]
+    left = [(i, (i - 1) % size) for i in range(size)]
+    out = jnp.zeros((*white.shape[:1], size * rows_2, *white.shape[1 + 1 :]), white.dtype)
+    out = lax.dynamic_update_slice_in_dim(out, white, index * rows_2, axis=1)
+    from_left = from_right = white
+    half = size // 2
+    for step in range(1, half + 1):
+        from_left = lax.ppermute(from_left, "ch", forward_2)
+        out = lax.dynamic_update_slice_in_dim(
+            out, from_left, (index - step) % size * rows_2, axis=1
+        )
+        if step < size - half:
+            from_right = lax.ppermute(from_right, "ch", left)
+            out = lax.dynamic_update_slice_in_dim(
+                out, from_right, (index + step) % size * rows_2, axis=1
+            )
+    gathered = out
     pair_codes = pair_list[0]
     partial_value = lax.map(
         lambda pair_entry: cross_block(gathered, pair_entry, BLK, NB), pair_codes

time: 476 us -> 505 us (1.061)
  starting transfers between devices: 0.22 us -> 19.9 us
  local copies, waits for them, and re-layouts: 30.2 us -> 39.9 us
    ppermute x0 -> x7, waiting for transfers between devices: none -> 128 us  [the longest x4 128 us: local(): from_left = lax.ppermute(from_left, 'ch', forward_2)]
    all_gather x1 -> x0, waiting for transfers between devices: 128 us -> none  [local(): gathered = lax.all_gather(white, 'ch', axis=1, tiled=True)]
    ppermute x0 -> x7, starting transfers between devices: none -> 19.9 us  [the longest x4 10.6 us: local(): from_left = lax.ppermute(from_left, 'ch', forward_2)]
    while x1 -> x0, local copies, waits for them, and re-layouts: 11.7 us -> none  [local(): lax.map(lambda pair_entry: cross_block(gathered, pair_entry, BLK, NB), pa...]
    dynamic_update_slice x0 -> x8, local copies, waits for them, and re-layouts: none -> 8.66 us  [the longest x4 4.36 us: local(): lax.dynamic_update_slice_in_dim(out, from_left, (index - step) % size * r...]
    ppermute x0 -> x7, local copies, waits for them, and re-layouts: none -> 7.51 us  [the longest x4 4.02 us: local(): from_left = lax.ppermute(from_left, 'ch', forward_2)]
  transfers between devices with their start and end apart: 2 -> 8, of which waited for: 2 -> 5; matrix products, arithmetic and copies ran while one was open for 14% -> 17% of each run, Pallas kernels for 0% -> 0%
where the time goes in v1:
time: 505 us
  waiting for transfers between devices  211 us (42%)
  other arithmetic  161 us (32%)
  matrix products  51.5 us (10%)
  local copies, waits for them, and re-layouts  39.9 us (8%)
  starting transfers between devices  19.9 us (4%)
  between operations  13.6 us (3%)
  loops' own time  8.19 us (2%)
    ppermute x4, waiting for transfers between devices, local(): from_left = lax.ppermute(from_left, 'ch', forward_2)  128 us
    psum x1, waiting for transfers between devices, local(): summed = lax.psum(flat_partial, 'grp')  83 us
    another operation x1, other arithmetic  69.9 us
    cos x1, other arithmetic, inverse_table(): return jnp.concatenate([jnp.cos(angles), -jnp.sin(angles)], axis=0)  68.4 us
    dot_general x1, matrix products, local(): jnp.dot(total.reshape(-1, 2 * NB), inverse, precision=lax.Precision.HIGHE...  34.3 us
    convert_element_type x6, other arithmetic, cross_block(): lax.dynamic_slice_in_dim(rows, pair_entry[0] * block, block, 1)  11.3 us
    ppermute x4, starting transfers between devices, local(): from_left = lax.ppermute(from_left, 'ch', forward_2)  10.6 us
  transfers between devices with their start and end apart: 8, of which 5 were waited for; matrix products, arithmetic and copies ran while one was open for 17% of the time, Pallas kernels for 0%

profile of v1, /device:TPU:0, one launch (start us, length us, event | category | flops | bytes accessed | tf_op | source)
XLA Modules:
  0.0 504.8 jit_solution(5393247847474710143)
XLA Ops:
  6.6 0.8 convert_element_type.43
  7.4 69.9 %multiply_convert_fusion.1 = (bf16[4096,1024]{1,0:T(8,128)(2,1)}, bf16[4096,1024]{1,0:T(8,128)(2,1)}) fusion(s32[1024]{0:T(1024)S(1)} %iota_add_fusion.1, f32[4096]{0:T(1024)S(1)} %get-tuple-element.46, f32[4096]{0:T(1024)S(1)} %get-tuple-element.47), kind=kLoop, calls=%fused_computation.31 | loop fusion | flops 75497472 | bytes 16814080 | tf_op jit(solution)/shard_map/convert
  77.4 9.8 %fusion.11 = f32[2048,256]{0,1:T(8,128)} fusion(bf16[256,4096]{1,0:T(8,128)(2,1)S(1)} %bitcast.29, bf16[4096,1024]{1,0:T(8,128)(2,1)} %get-tuple-element.45, bf16[4096,1024]{1,0:T(8,128)(2,1)} %get-tuple-element.44), kind=kOutput, calls=%fused_computation.25 | convolution fusion | flops 4328521728 | bytes 20971520 | tf_op jit(solution)/shard_map/dot_general | solution.py:63
  87.2 1.9 copy.18
  89.7 3.0 collective-permute-start
  92.8 3.1 collective-permute-start.1
  95.9 41.8 %collective-permute-done = bf16[2,128,2048]{1,2,0:T(8,128)(2,1)S(1)} collective-permute-done((bf16[2,128,2048]{1,2,0:T(8,128)(2,1)S(1)}, bf16[2,128,2048]{1,2,0:T(8,128)(2,1)S(1)}, u32[]{:S(2)}, u32[]{:S(2)}) %collective-permute-start) | collective-permute-done | bytes 1048608 | tf_op jit(solution)/shard_map/ppermute | solution.py:74
  137.6 2.5 collective-permute-start.2
  140.1 3.1 collective-permute-start.3
  143.2 40.9 %collective-permute-done.2 = bf16[2,128,2048]{1,2,0:T(8,128)(2,1)} collective-permute-done((bf16[2,128,2048]{1,2,0:T(8,128)(2,1)S(1)}, bf16[2,128,2048]{1,2,0:T(8,128)(2,1)}, u32[]{:S(2)}, u32[]{:S(2)}) %collective-permute-start.2) | collective-permute-done | bytes 1048608 | tf_op jit(solution)/shard_map/ppermute | solution.py:74
  184.2 2.6 collective-permute-start.4
  187.3 3.1 collective-permute-start.5
  190.4 4.3 broadcast_in_dim.11
  194.7 1.1 constant_dynamic-update-slice_fusion.7
  196.9 1.1 constant_dynamic-update-slice_fusion.6
  198.0 32.4 %collective-permute-done.4 = bf16[2,128,2048]{1,2,0:T(8,128)(2,1)} collective-permute-done((bf16[2,128,2048]{1,2,0:T(8,128)(2,1)}, bf16[2,128,2048]{1,2,0:T(8,128)(2,1)}, u32[]{:S(2)}, u32[]{:S(2)}) %collective-permute-start.4) | collective-permute-done | bytes 1048608 | tf_op jit(solution)/shard_map/ppermute | solution.py:74
  230.4 2.5 collective-permute-start.6
  232.9 1.1 constant_dynamic-update-slice_fusion.5
  234.0 1.5 copy.23
  235.4 1.5 copy.22
  236.9 1.1 constant_dynamic-update-slice_fusion.4
  238.0 1.1 constant_dynamic-update-slice_fusion.3
  239.1 1.5 copy.24
  240.6 1.5 copy.25
  242.1 1.1 constant_dynamic-update-slice_fusion.2
  243.2 1.1 constant_dynamic-update-slice_fusion.1
  244.2 12.5 %collective-permute-done.6 = bf16[2,128,2048]{1,2,0:T(8,128)(2,1)S(1)} collective-permute-done((bf16[2,128,2048]{1,2,0:T(8,128)(2,1)}, bf16[2,128,2048]{1,2,0:T(8,128)(2,1)S(1)}, u32[]{:S(2)}, u32[]{:S(2)}) %collective-permute-start.6) | collective-permute-done | bytes 1048608 | tf_op jit(solution)/shard_map/ppermute | solution.py:74
  257.3 1.1 constant_dynamic-update-slice_fusion
  258.3 33.3 %while.10 = (s32[]{:T(128)}, f32[6,128,2048]{2,1,0:T(8,128)}, s32[6,2]{0,1:T(2,128)S(1)}, bf16[2,1024,2048]{2,1,0:T(8,128)(2,1)}, s32[]{:T(128)}, /*index=5*/s32[1,1]{0,1:T(1,128)}, s32[]{:T(128)}, s32[]{:T(128)}) while((s32[]{:T(128)}, f32[6,128,2048]{2,1,0:T(8,128)}, s32[6,2]{0,1:T(2,128)S(1)}, bf16[2,1024,2048]{2,1,0:T(8,128)(2,1)}, ...), condition=%wide.region_5.6_spmd, body=%wide.region_2.5_spmd.sunk | while | flops 3145738 | bytes 13631721 | solution.py:85
  258.4 0.6 fusion.41
  260.4 1.9 dynamic-slice_convert_fusion.3
  262.8 1.1 fusion.42
  266.0 1.9 dynamic-slice_convert_fusion.3
  268.4 1.0 fusion.42
  271.5 1.9 dynamic-slice_convert_fusion.3
  273.9 1.1 fusion.42
  277.0 1.9 dynamic-slice_convert_fusion.3
  279.5 1.1 fusion.42
  282.6 1.9 dynamic-slice_convert_fusion.3
  285.0 1.1 fusion.42
  288.2 1.9 dynamic-slice_convert_fusion.3
  290.6 1.1 fusion.42
  291.7 9.8 %copy.27 = f32[1,6,128,2048]{3,1,2,0:T(8,128)} copy(f32[1,6,128,2048]{3,2,1,0:T(8,128)} %bitcast.31) | data formatting | bytes 12582912
  301.7 68.4 %fusion.18 = (f32[1024,4096]{1,0:T(8,128)}, f32[1024,4096]{1,0:T(8,128)}) fusion(s32[4096]{0:T(1024)S(1)} %iota_add_fusion, s32[1024]{0:T(1024)S(1)} %iota_add_fusion.1), kind=kLoop, calls=%fused_computation.35 | loop fusion | flops 62914560 | bytes 33574912 | tf_op jit(solution)/shard_map/cos | solution.py:32
  370.1 83.0 %all-reduce.2.cloned.1.call-done = f32[6,262144]{1,0:T(8,128)} async-done(((f32[6,262144]{1,0:T(8,128)}), f32[6,262144]{1,0:T(8,128)}) %all-reduce.2.cloned.1.call-update) | async-done | bytes 6291472 | tf_op jit(solution)/shard_map/psum | solution.py:95
  453.1 7.4 %fusion.27 = f32[2,262144]{1,0:T(2,128)S(1)} fusion(f32[6,262144]{1,0:T(8,128)} %all-reduce.2.cloned.1.call-done, pred[6]{0:T(512)(128)(4,1)S(1)} %compare_bitcast_fusion, s32[6]{0:T(128)S(1)} %convert_reduce_fusion), kind=kOutput, calls=%fused_computation.60 | convolution fusion | flops 37748760 | bytes 8388638 | tf_op jit(solution)/shard_map/dot_general | solution.py:100
  460.6 3.1 reshape.62
  463.7 34.3 %fusion.19 = f32[256,4096]{1,0:T(8,128)} fusion(f32[256,2048]{1,0:T(8,128)} %reshape.62, f32[1024,4096]{1,0:T(8,128)} %get-tuple-element.43, f32[1024,4096]{1,0:T(8,128)} %get-tuple-element.42), kind=kOutput, calls=%fused_computation.36 | convolution fusion | flops 25779240960 | bytes 39845888 | tf_op jit(solution)/shard_map/dot_general | solution.py:104
  (48 shorter events, 9.8 us)
Async XLA Ops:
  6.5 70.8 %copy-start = (bf16[2,128,4096]{2,1,0:T(8,128)(2,1)S(1)}, bf16[2,128,4096]{2,1,0:T(8,128)(2,1)}, u32[]{:S(2)}) copy-start(bf16[2,128,4096]{2,1,0:T(8,128)(2,1)} %param.6) | copy-start | bytes 6291460
  6.5 446.6 %all-reduce.2.cloned.1.call-start = ((), (), s32[]{:S(2)}) async-start(), calls=%async_computation | async-start | bytes 16777216 | tf_op jit(solution)/shard_map/psum | solution.py:95
  89.7 47.9 %collective-permute-start = (bf16[2,128,2048]{1,2,0:T(8,128)(2,1)S(1)}, bf16[2,128,2048]{1,2,0:T(8,128)(2,1)S(1)}, u32[]{:S(2)}, u32[]{:S(2)}) collective-permute-start(bf16[2,128,2048]{1,2,0:T(8,128)(2,1)S(1)} %fusion.23), channel_id=1, source_target_pairs={{0,1},{1,2},{2,3},{3,4},{4,5},{5,6},{6,7},{7,0},{8,9},{9,10},{10,1... | collective-permute-start | bytes 3145736 | tf_op jit(solution)/shard_map/ppermute | solution.py:74
  92.8 47.4 %collective-permute-start.1 = (bf16[2,128,2048]{1,2,0:T(8,128)(2,1)S(1)}, bf16[2,128,2048]{1,2,0:T(8,128)(2,1)S(1)}, u32[]{:S(2)}, u32[]{:S(2)}) collective-permute-start(bf16[2,128,2048]{1,2,0:T(8,128)(2,1)S(1)} %fusion.23), channel_id=1, source_target_pairs={{0,7},{1,0},{2,1},{3,2},{4,3},{5,4},{6,5},{7,6},{8,15},{9,8},{10,9... | collective-permute-start | bytes 3145736 | tf_op jit(solution)/shard_map/ppermute | solution.py:79
  137.6 49.1 %copy-start.2 = (bf16[2,128,2048]{1,2,0:T(8,128)(2,1)}, bf16[2,128,2048]{1,2,0:T(8,128)(2,1)S(1)}, u32[]{:S(2)}) copy-start(bf16[2,128,2048]{1,2,0:T(8,128)(2,1)S(1)} %collective-permute-done) | copy-start | bytes 3145732
  137.6 46.5 %collective-permute-start.2 = (bf16[2,128,2048]{1,2,0:T(8,128)(2,1)S(1)}, bf16[2,128,2048]{1,2,0:T(8,128)(2,1)}, u32[]{:S(2)}, u32[]{:S(2)}) collective-permute-start(bf16[2,128,2048]{1,2,0:T(8,128)(2,1)S(1)} %collective-permute-done), channel_id=1, source_target_pairs={{0,1},{1,2},{2,3},{3,4},{4,5},{5,6},{6,7},{7,0},{8,9},{9,10},{10,1... | collective-permute-start | bytes 3145736 | tf_op jit(solution)/shard_map/ppermute | solution.py:74
  140.1 47.2 %collective-permute-start.3 = (bf16[2,128,2048]{1,2,0:T(8,128)(2,1)S(1)}, bf16[2,128,2048]{1,2,0:T(8,128)(2,1)}, u32[]{:S(2)}, u32[]{:S(2)}) collective-permute-start(bf16[2,128,2048]{1,2,0:T(8,128)(2,1)S(1)} %collective-permute-done.1), channel_id=1, source_target_pairs={{0,7},{1,0},{2,1},{3,2},{4,3},{5,4},{6,5},{7,6},{8,15},{9,8},{10,9... | collective-permute-start | bytes 3145736 | tf_op jit(solution)/shard_map/ppermute | solution.py:79
  184.2 46.2 %collective-permute-start.4 = (bf16[2,128,2048]{1,2,0:T(8,128)(2,1)}, bf16[2,128,2048]{1,2,0:T(8,128)(2,1)}, u32[]{:S(2)}, u32[]{:S(2)}) collective-permute-start(bf16[2,128,2048]{1,2,0:T(8,128)(2,1)} %collective-permute-done.2), channel_id=1, source_target_pairs={{0,1},{1,2},{2,3},{3,4},{4,5},{5,6},{6,7},{7,0},{8,9},{9,10},{10,1... | collective-permute-start | bytes 3145736 | tf_op jit(solution)/shard_map/ppermute | solution.py:74
  187.3 9.0 %copy-start.3 = (bf16[2,128,2048]{1,2,0:T(8,128)(2,1)S(1)}, bf16[2,128,2048]{1,2,0:T(8,128)(2,1)}, u32[]{:S(2)}) copy-start(bf16[2,128,2048]{1,2,0:T(8,128)(2,1)} %copy-done.2) | copy-start | bytes 3145732
  187.3 53.3 %collective-permute-start.5 = (bf16[2,128,2048]{1,2,0:T(8,128)(2,1)}, bf16[2,128,2048]{1,2,0:T(8,128)(2,1)}, u32[]{:S(2)}, u32[]{:S(2)}) collective-permute-start(bf16[2,128,2048]{1,2,0:T(8,128)(2,1)} %collective-permute-done.3), channel_id=1, source_target_pairs={{0,7},{1,0},{2,1},{3,2},{4,3},{5,4},{6,5},{7,6},{8,15},{9,8},{10,9... | collective-permute-start | bytes 3145736 | tf_op jit(solution)/shard_map/ppermute | solution.py:79
  230.4 26.3 %collective-permute-start.6 = (bf16[2,128,2048]{1,2,0:T(8,128)(2,1)}, bf16[2,128,2048]{1,2,0:T(8,128)(2,1)S(1)}, u32[]{:S(2)}, u32[]{:S(2)}) collective-permute-start(bf16[2,128,2048]{1,2,0:T(8,128)(2,1)} %collective-permute-done.4), channel_id=1, source_target_pairs={{0,1},{1,2},{2,3},{3,4},{4,5},{5,6},{6,7},{7,0},{8,9},{9,10},{10,1... | collective-permute-start | bytes 3145736 | tf_op jit(solution)/shard_map/ppermute | solution.py:74
  236.9 21.4 %copy-start.4 = (s32[1,6,2]{1,2,0:T(2,128)S(1)}, s32[1,6,2]{1,2,0:T(2,128)}, u32[]{:S(2)}) copy-start(s32[1,6,2]{1,2,0:T(2,128)} %param.8) | copy-start | bytes 148
  291.7 9.8 %copy-start.5 = (s32[1,6]{1,0:T(1,128)S(1)}, s32[1,6]{1,0:T(1,128)}, u32[]{:S(2)}) copy-start(s32[1,6]{1,0:T(1,128)} %param.9) | copy-start | bytes 76
  463.7 34.3 %copy-start.1 = (bf16[2,128,4096]{2,1,0:T(8,128)(2,1)S(1)}, bf16[2,128,4096]{2,1,0:T(8,128)(2,1)}, u32[]{:S(2)}) copy-start(bf16[2,128,4096]{2,1,0:T(8,128)(2,1)} %param.6) | copy-start | bytes 6291460
Sparse Core Ops, SparseCore 0:
  301.6 151.4 all-reduce.1
